TPU v7x, 256 devices: a whole 4x4x8 slice. The times are simulated.
256 devices in a mesh: seq: 32 (over z, y), head: 8 (over x, core).
Axes of the slice: x: 4, y: 4, z: 8, core: 2. Of those that a mesh axis runs over, the one named last changes fastest.
Arguments:
- query: bfloat16 [16384, 6144], P('seq', 'head'), may hold values from -6 to 6
- key: bfloat16 [16384, 6144], P('seq', 'head'), may hold values from -6 to 6
- value: bfloat16 [16384, 6144], P('seq', 'head'), may hold values from -6 to 6
- init_state: float32 [48, 128, 128], P('head'), may hold values from -768 to 768
- out_weight: bfloat16 [6144, 6144], P(('head', 'seq')), may hold values from -0.078125 to 0.078125
- out_grad: bfloat16 [16384, 6144], P('seq'), may hold values from -24 to 24
Outputs:
- mixed: bfloat16 [16384, 6144], P('seq', 'head')
- grad_query: bfloat16 [16384, 6144], P('seq', 'head')
- grad_key: bfloat16 [16384, 6144], P('seq', 'head')
- grad_value: bfloat16 [16384, 6144], P('seq', 'head')
- init_grad: float32 [48, 128, 128], P('head')
All inputs are finite; a program needn't handle non-finite values.
Results may differ from a plain program's by a relative error of at most 0.017.
Values may be sent and summed in bfloat16 or wider, within the bound.
A program may use at most 128 MiB of HBM per device.

v0:
```python
import jax
import jax.numpy as jnp
from jax import lax
from jax.sharding import PartitionSpec as P

EPS = 1e-06


def prefix(value, axis, join, neutral, backward):
    count = lax.axis_size(axis)
    place = lax.axis_index(axis)
    ahead = count - 1 - place if backward else place
    gathered = lax.all_gather(value.astype(jnp.bfloat16), axis)
    state = jnp.zeros_like(value) + jnp.asarray(neutral, value.dtype)

    def one(turn, state):
        source = count - 1 - turn if backward else turn
        return join(state, lax.dynamic_index_in_dim(gathered, source, 0, False).astype(value.dtype))

    return lax.fori_loop(0, ahead, one, state)


def normalize(attended):
    return attended * lax.rsqrt(jnp.mean(attended * attended, axis=-1, keepdims=True) + EPS)


def add_states(earlier, later):
    return earlier + later


def shards(query, key, value, init_state, out_weight, out_grad):
    tok_rows = query.shape[0]
    width = query.shape[1]
    heads_here = init_state.shape[0]
    head_dim = init_state.shape[2]
    queries = query.reshape(tok_rows, heads_here, head_dim)
    key_rows = key.reshape(tok_rows, heads_here, head_dim)
    val_rows = value.reshape(tok_rows, heads_here, head_dim)
    local_state = jnp.einsum("thi,thj->hij", key_rows, val_rows, preferred_element_type=jnp.float32)
    zero_state = jnp.zeros_like(local_state)
    earlier = prefix(local_state, "seq", add_states, zero_state, False)
    state_half = (init_state + earlier).astype(jnp.bfloat16)
    row_index = lax.broadcasted_iota(jnp.int32, (tok_rows, tok_rows), 0)
    col_index = lax.broadcasted_iota(jnp.int32, (tok_rows, tok_rows), 1)
    causal = col_index <= row_index
    scores = jnp.einsum("thi,shi->hts", queries, key_rows, preferred_element_type=jnp.float32)
    attn_weights = jnp.where(causal, scores, 0.0).astype(jnp.bfloat16)
    attended = jnp.einsum(
        "hts,shj->thj", attn_weights, val_rows, preferred_element_type=jnp.float32
    )
    attended = attended + jnp.einsum(
        "thi,hij->thj", queries, state_half, preferred_element_type=jnp.float32
    )
    normed = normalize(attended).astype(jnp.bfloat16).reshape(tok_rows, width)
    weight_rows = lax.all_gather(out_weight, "seq", axis=0, tiled=True)
    projected = jnp.dot(normed, weight_rows, preferred_element_type=jnp.float32)
    grad_normed = lax.dot_general(
        out_grad, weight_rows, (((1,), (1,)), ((), ())), preferred_element_type=jnp.float32
    )
    mixed = lax.psum_scatter(
        projected.astype(jnp.bfloat16), "head", scatter_dimension=1, tiled=True
    )
    _, norm_back = jax.vjp(normalize, attended)
    grad_att = norm_back(grad_normed.reshape(tok_rows, heads_here, head_dim))[0].astype(
        jnp.bfloat16
    )
    grad_scores = jnp.einsum("thj,shj->hts", grad_att, val_rows, preferred_element_type=jnp.float32)
    grad_scores = jnp.where(causal, grad_scores, 0.0).astype(jnp.bfloat16)
    own_adjoint = jnp.einsum("thi,thj->hij", queries, grad_att, preferred_element_type=jnp.float32)
    later = prefix(own_adjoint, "seq", add_states, zero_state, True)
    later_half = later.astype(jnp.bfloat16)
    grad_query = jnp.einsum(
        "hts,shi->thi", grad_scores, key_rows, preferred_element_type=jnp.float32
    )
    grad_query = grad_query + jnp.einsum(
        "thj,hij->thi", grad_att, state_half, preferred_element_type=jnp.float32
    )
    grad_key = jnp.einsum("hts,thi->shi", grad_scores, queries, preferred_element_type=jnp.float32)
    grad_key = grad_key + jnp.einsum(
        "thj,hij->thi", val_rows, later_half, preferred_element_type=jnp.float32
    )
    grad_value = jnp.einsum(
        "hts,thj->shj", attn_weights, grad_att, preferred_element_type=jnp.float32
    )
    grad_value = grad_value + jnp.einsum(
        "thi,hij->thj", key_rows, later_half, preferred_element_type=jnp.float32
    )
    init_grad = lax.psum(own_adjoint.astype(jnp.bfloat16), "seq").astype(jnp.float32)
    return (
        mixed,
        grad_query.reshape(tok_rows, width).astype(jnp.bfloat16),
        grad_key.reshape(tok_rows, width).astype(jnp.bfloat16),
        grad_value.reshape(tok_rows, width).astype(jnp.bfloat16),
        init_grad,
    )


def solution(mesh):
    return jax.shard_map(
        shards,
        mesh=mesh,
        in_specs=(
            P("seq", "head"),
            P("seq", "head"),
            P("seq", "head"),
            P("head", None, None),
            P(("head", "seq"), None),
            P("seq", None),
        ),
        out_specs=(
            P("seq", "head"),
            P("seq", "head"),
            P("seq", "head"),
            P("seq", "head"),
            P("head", None, None),
        ),
        check_vma=False,
    )
```

profile of v0, /device:TPU:1, one launch (start us, length us, event | category | flops | bytes accessed | tf_op | source)
XLA Modules:
  0.0 504.5 jit_solution(3683059020974468242)
XLA Ops:
  7.2 1.5 copy.55
  8.7 1.4 copy.58
  10.1 1.0 convolution_convert_fusion.2
  12.3 1.1 select_convert_fusion.1
  13.5 1.7 copy-done
  15.1 2.3 fusion.7
  17.4 86.1 %all-gather.8.cloned.1.call-done = bf16[192,128,128]{2,1,0:T(8,128)(2,1)} async-done(((bf16[6,128,128]{2,1,0:T(8,128)(2,1)}), bf16[192,128,128]{2,1,0:T(8,128)(2,1)}) %all-gather.8.cloned.1.call-update) | async-done | bytes 6291472 | tf_op jit(solution)/shard_map/all_gather | solution.py:13
  103.6 102.9 %all-gather.6.cloned.1.call-done = bf16[768,6144]{1,0:T(8,128)(2,1)} async-done(((bf16[24,6144]{1,0:T(8,128)(2,1)}), bf16[768,6144]{1,0:T(8,128)(2,1)}) %all-gather.6.cloned.1.call-update) | async-done | bytes 9437200 | tf_op jit(solution)/shard_map/all_gather | solution.py:55
  206.5 9.6 %fusion.8 = f32[512,768]{0,1:T(8,128)S(1)} fusion(bf16[512,6144]{1,0:T(8,128)(2,1)} %param.15, bf16[768,6144]{1,0:T(8,128)(2,1)} %all-gather.6.cloned.1.call-done), kind=kOutput, calls=%fused_computation.27 | convolution fusion | flops 4831838208 | bytes 17301504 | tf_op jit(solution)/shard_map/dot_general | solution.py:57
  216.8 1.4 fusion
  220.9 10.8 %convolution_convert_fusion = bf16[512,6144]{1,0:T(8,128)(2,1)} fusion(bf16[512,768]{0,1:T(8,128)(2,1)} %bitcast.83, bf16[768,6144]{1,0:T(8,128)(2,1)} %all-gather.6.cloned.1.call-done), kind=kOutput, calls=%fused_computation.2 | convolution fusion | flops 4834983936 | bytes 16515072 | tf_op jit(solution)/shard_map/dot_general | solution.py:56
  231.7 2.0 select_convert_fusion
  233.8 1.1 fusion.9
  234.9 1.2 fusion.2
  236.2 2.3 copy.71
  238.5 3.8 fusion.10
  242.2 1.8 fusion.11
  244.0 115.4 %all-reduce.2.cloned.1.call-done = bf16[6,128,128]{1,2,0:T(8,128)(2,1)} async-done(((bf16[6,128,128]{1,2,0:T(8,128)(2,1)}), bf16[6,128,128]{1,2,0:T(8,128)(2,1)}) %all-reduce.2.cloned.1.call-update) | async-done | bytes 196624 | tf_op jit(solution)/shard_map/psum | solution.py:88
  359.4 1.8 copy.74
  361.2 91.8 %all-gather.10.cloned.1.call-done = bf16[192,128,128]{2,1,0:T(8,128)(2,1)} async-done(((bf16[6,128,128]{2,1,0:T(8,128)(2,1)}), bf16[192,128,128]{2,1,0:T(8,128)(2,1)}) %all-gather.10.cloned.1.call-update) | async-done | bytes 6291472 | tf_op jit(solution)/shard_map/all_gather | solution.py:13
  453.0 32.2 %while.23 = (s32[]{:T(128)}, f32[6,128,128]{2,1,0:T(8,128)S(1)}, s32[]{:T(128)}, bf16[32,6,128,128]{3,2,1,0:T(8,128)(2,1)}, s32[]{:T(128)}, /*index=5*/s32[]{:T(128)}, s32[]{:T(128)}, s32[]{:T(128)}) while((s32[]{:T(128)}, f32[6,128,128]{2,1,0:T(8,128)S(1)}, s32[]{:T(128)}, bf16[32,6,128,128]{3,2,1,0:T(8,128)(2,1)}, s32[]{:T(128)}, ...), condition=%wide.region_6.7_spmd, body=%wide.region_5.6_spmd.sunk | while | flops 196614 | bytes 983183 | solution.py:20
  453.1 1.0 convert_add_fusion.5
  457.2 1.0 convert_add_fusion.5
  458.2 1.0 convert_add_fusion.5
  463.4 1.0 convert_add_fusion.5
  464.4 1.1 convert_add_fusion.5
  465.5 1.0 convert_add_fusion.5
  467.6 1.0 convert_add_fusion.5
  468.6 1.0 convert_add_fusion.5
  469.7 1.0 convert_add_fusion.5
  470.7 1.0 convert_add_fusion.5
  471.7 1.0 convert_add_fusion.5
  472.8 1.0 convert_add_fusion.5
  473.8 1.0 convert_add_fusion.5
  474.9 1.0 convert_add_fusion.5
  475.9 1.0 convert_add_fusion.5
  476.9 1.0 convert_add_fusion.5
  478.0 1.0 convert_add_fusion.5
  479.0 1.0 convert_add_fusion.5
  480.1 1.0 convert_add_fusion.5
  481.1 1.0 convert_add_fusion.5
  482.1 1.0 convert_add_fusion.5
  483.2 1.0 convert_add_fusion.5
  484.2 1.0 convert_add_fusion.5
  485.3 2.9 add_convert_fusion
  488.1 2.3 copy.73
  490.8 1.2 copy.72
  491.9 6.0 %reduce-scatter.2.cloned.1.call-done = bf16[512,768]{1,0:T(8,128)(2,1)} async-done(((bf16[512,6144]{1,0:T(8,128)(2,1)}), bf16[512,768]{1,0:T(8,128)(2,1)}) %reduce-scatter.2.cloned.1.call-update) | async-done | bytes 786448 | tf_op jit(solution)/shard_map/reduce_scatter | solution.py:60
  (46 shorter events, 13.0 us)
Async XLA Ops:
  7.2 4.8 copy-start.6
  7.2 96.3 %all-gather.8.cloned.1.call-start = ((), (), s32[]{:S(2)}) async-start(), calls=%async_computation.4 | async-start | bytes 6488064 | tf_op jit(solution)/shard_map/all_gather | solution.py:13
  11.2 195.4 %all-gather.6.cloned.1.call-start = ((), (), s32[]{:S(2)}) async-start(), calls=%async_computation.1 | async-start | bytes 9732096 | tf_op jit(solution)/shard_map/all_gather | solution.py:55
  12.3 1.1 copy-start.8
  13.4 1.7 copy-start
  17.4 86.2 %copy-start.7 = (f32[6,128,128]{2,1,0:T(8,128)S(1)}, f32[6,128,128]{2,1,0:T(8,128)}, u32[]{:S(2)}) copy-start(f32[6,128,128]{2,1,0:T(8,128)} %param.13) | copy-start | bytes 1179652
  206.5 9.6 %copy-start.4 = (f32[6,512,128]{1,2,0:T(8,128)S(1)}, f32[6,512,128]{1,2,0:T(8,128)}, u32[]{:S(2)}) copy-start(f32[6,512,128]{1,2,0:T(8,128)} %fusion.7) | copy-start | bytes 4718596
  218.5 0.8 copy-start.5
  219.4 140.0 %all-reduce.2.cloned.1.call-start = ((), (), s32[]{:S(2)}) async-start(), calls=%async_computation.3 | async-start | bytes 393216 | tf_op jit(solution)/shard_map/psum | solution.py:88
  220.1 232.9 %all-gather.10.cloned.1.call-start = ((), (), s32[]{:S(2)}) async-start(), calls=%async_computation.5 | async-start | bytes 6488064 | tf_op jit(solution)/shard_map/all_gather | solution.py:13
  220.7 277.3 %reduce-scatter.2.cloned.1.call-start = ((), (), s32[]{:S(2)}) async-start(), calls=%async_computation.2 | async-start | bytes 7077888 | tf_op jit(solution)/shard_map/reduce_scatter | solution.py:60
  233.8 2.4 copy-start.1
  238.4 3.8 copy-start.2
  485.3 5.2 %copy-start.3 = (f32[6,512,128]{1,2,0:T(8,128)S(1)}, f32[6,512,128]{1,2,0:T(8,128)}, u32[]{:S(2)}) copy-start(f32[6,512,128]{1,2,0:T(8,128)} %fusion.11) | copy-start | bytes 4718596
Sparse Core Ops, SparseCore 0:
  11.3 92.1 all-gather.7
  106.1 100.4 all-gather.5
  223.6 135.7 all-reduce.1
  362.7 90.2 all-gather.9
  456.1 41.7 reduce-scatter.1
where the time goes:
time: 506 us; the launch traced here: 504 us
  waiting for transfers between devices  404 us (80%)
  matrix products  38.9 us (8%)
  other arithmetic  33 us (7%)
  between operations  14 us (3%)
  local copies, waits for them, and re-layouts  13.3 us (3%)
    all_gather x2, waiting for transfers between devices, prefix(): gathered = lax.all_gather(value.astype(jnp.bfloat16), axis)  178 us
    psum x1, waiting for transfers between devices, shards(): lax.psum(own_adjoint.astype(jnp.bfloat16), 'seq').astype(jnp.float32)  115 us
    all_gather x1, waiting for transfers between devices, shards(): weight_rows = lax.all_gather(out_weight, 'seq', axis=0, tiled=True)  103 us
    add x31, other arithmetic, add_states(): return earlier + later  31.5 us
    unnamed x25, local copies, waits for them, and re-layouts  12.4 us
    dot_general x1, matrix products, shards(): projected = jnp.dot(normed, weight_rows, preferred_element_type=jnp.float32)  10.8 us
  transfers between devices with their start and end apart: 5, of which 5 were waited for; matrix products, arithmetic and copies ran while one was open for 13% of the time, Pallas kernels for 0%

commit v1 on v0

--- a/solution.py
+++ b/solution.py
@@ -85,7 +85,9 @@
     grad_value = grad_value + jnp.einsum(
         "thi,hij->thj", key_rows, later_half, preferred_element_type=jnp.float32
     )
-    init_grad = lax.psum(own_adjoint.astype(jnp.bfloat16), "seq").astype(jnp.float32)
+    init_grad = jnp.sum(lax.all_gather(own_adjoint.astype(jnp.bfloat16), "seq"), axis=0).astype(
+        jnp.float32
+    )
     return (
         mixed,
         grad_query.reshape(tok_rows, width).astype(jnp.bfloat16),

time: 506 us -> 358 us (0.71)
  waiting for transfers between devices: 404 us -> 255 us
    psum x1 -> x0, waiting for transfers between devices: 115 us -> none  [shards(): lax.psum(own_adjoint.astype(jnp.bfloat16), 'seq').astype(jnp.float32)]
    all_gather x2, waiting for transfers between devices: 178 us -> 149 us  [prefix(): gathered = lax.all_gather(value.astype(jnp.bfloat16), axis)]
    unnamed x25 -> x24, local copies, waits for them, and re-layouts: 12.4 us -> 10.5 us
  transfers between devices with their start and end apart: 5 -> 4, of which waited for: 5 -> 4; matrix products, arithmetic and copies ran while one was open for 13% -> 19% of each run, Pallas kernels for 0% -> 0%
where the time goes in v1:
time: 358 us; the launch traced here: 357 us
  waiting for transfers between devices  255 us (71%)
  matrix products  37.9 us (11%)
  other arithmetic  37.5 us (10%)
  between operations  13.9 us (4%)
  local copies, waits for them, and re-layouts  11.4 us (3%)
    all_gather x2, waiting for transfers between devices, prefix(): gathered = lax.all_gather(value.astype(jnp.bfloat16), axis)  149 us
    all_gather x1, waiting for transfers between devices, shards(): weight_rows = lax.all_gather(out_weight, 'seq', axis=0, tiled=True)  103 us
    add x31, other arithmetic, add_states(): return earlier + later  31.5 us
    dot_general x1, matrix products, shards(): projected = jnp.dot(normed, weight_rows, preferred_element_type=jnp.float32)  10.8 us
    unnamed x24, local copies, waits for them, and re-layouts  10.5 us
    dot_general x1, matrix products, shards(): lax.dot_general(out_grad, weight_rows, (((1,), (1,)), ((), ())), preferre...  9.62 us
  transfers between devices with their start and end apart: 4, of which 4 were waited for; matrix products, arithmetic and copies ran while one was open for 19% of the time, Pallas kernels for 0%

profile of v1, /device:TPU:1, one launch (start us, length us, event | category | flops | bytes accessed | tf_op | source)
XLA Modules:
  0.0 356.7 jit_solution(5584453741933214239)
XLA Ops:
  7.2 1.5 copy.53
  8.7 1.4 copy.56
  10.1 1.0 convolution_convert_fusion.2
  12.4 1.1 select_convert_fusion.1
  13.5 1.7 copy-done
  15.2 2.3 fusion.7
  17.4 86.1 %all-gather.8.cloned.1.call-done = bf16[192,128,128]{2,1,0:T(8,128)(2,1)} async-done(((bf16[6,128,128]{2,1,0:T(8,128)(2,1)}), bf16[192,128,128]{2,1,0:T(8,128)(2,1)}) %all-gather.8.cloned.1.call-update) | async-done | bytes 6291472 | tf_op jit(solution)/shard_map/all_gather | solution.py:13
  103.6 102.9 %all-gather.6.cloned.1.call-done = bf16[768,6144]{1,0:T(8,128)(2,1)} async-done(((bf16[24,6144]{1,0:T(8,128)(2,1)}), bf16[768,6144]{1,0:T(8,128)(2,1)}) %all-gather.6.cloned.1.call-update) | async-done | bytes 9437200 | tf_op jit(solution)/shard_map/all_gather | solution.py:55
  206.5 9.6 %fusion.8 = f32[512,768]{0,1:T(8,128)S(1)} fusion(bf16[512,6144]{1,0:T(8,128)(2,1)} %param.15, bf16[768,6144]{1,0:T(8,128)(2,1)} %all-gather.6.cloned.1.call-done), kind=kOutput, calls=%fused_computation.27 | convolution fusion | flops 4831838208 | bytes 17301504 | tf_op jit(solution)/shard_map/dot_general | solution.py:57
  216.8 1.4 fusion
  219.6 10.8 %convolution_convert_fusion = bf16[512,6144]{1,0:T(8,128)(2,1)} fusion(bf16[512,768]{0,1:T(8,128)(2,1)} %bitcast.84, bf16[768,6144]{1,0:T(8,128)(2,1)} %all-gather.6.cloned.1.call-done), kind=kOutput, calls=%fused_computation.2 | convolution fusion | flops 4834983936 | bytes 16515072 | tf_op jit(solution)/shard_map/dot_general | solution.py:56
  230.4 2.0 select_convert_fusion
  232.5 1.1 fusion.9
  233.6 1.2 fusion.2
  234.9 2.3 copy.70
  237.2 3.8 %fusion.10 = f32[6,128,512]{2,1,0:T(8,128)} fusion(bf16[512,6,128]{0,2,1:T(8,128)(2,1)S(1)} %get-tuple-element.127, bf16[6,512,512]{2,1,0:T(8,128)(2,1)} %copy-done), kind=kOutput, calls=%fused_computation.29 | convolution fusion | flops 402653184 | bytes 5505024 | tf_op jit(solution)/shard_map/hts,thj->shj/dot_general | solution.py:82
  241.0 1.8 fusion.11
  242.7 62.7 %all-gather.10.cloned.1.call-done = bf16[192,128,128]{2,1,0:T(8,128)(2,1)} async-done(((bf16[6,128,128]{2,1,0:T(8,128)(2,1)}), bf16[192,128,128]{2,1,0:T(8,128)(2,1)}) %all-gather.10.cloned.1.call-update) | async-done | bytes 6291472 | tf_op jit(solution)/shard_map/all_gather | solution.py:13
  305.4 32.2 %while.23 = (s32[]{:T(128)}, f32[6,128,128]{2,1,0:T(8,128)S(1)}, s32[]{:T(128)}, bf16[32,6,128,128]{3,2,1,0:T(8,128)(2,1)}, s32[]{:T(128)}, /*index=5*/s32[]{:T(128)}, s32[]{:T(128)}, s32[]{:T(128)}) while((s32[]{:T(128)}, f32[6,128,128]{2,1,0:T(8,128)S(1)}, s32[]{:T(128)}, bf16[32,6,128,128]{3,2,1,0:T(8,128)(2,1)}, s32[]{:T(128)}, ...), condition=%wide.region_6.7_spmd, body=%wide.region_5.6_spmd.sunk | while | flops 196614 | bytes 983183 | solution.py:20
  305.4 1.0 convert_add_fusion.5
  306.5 1.0 convert_add_fusion.5
  307.5 1.0 convert_add_fusion.5
  308.5 1.0 convert_add_fusion.5
  309.6 1.0 convert_add_fusion.5
  310.6 1.0 convert_add_fusion.5
  316.8 1.1 convert_add_fusion.5
  317.9 1.0 convert_add_fusion.5
  321.0 1.0 convert_add_fusion.5
  322.1 1.0 convert_add_fusion.5
  323.1 1.0 convert_add_fusion.5
  324.1 1.0 convert_add_fusion.5
  325.2 1.0 convert_add_fusion.5
  326.2 1.0 convert_add_fusion.5
  327.3 1.0 convert_add_fusion.5
  328.3 1.0 convert_add_fusion.5
  329.4 1.0 convert_add_fusion.5
  330.4 1.0 convert_add_fusion.5
  331.4 1.0 convert_add_fusion.5
  332.5 1.0 convert_add_fusion.5
  333.5 1.0 convert_add_fusion.5
  334.6 1.0 convert_add_fusion.5
  335.6 1.0 convert_add_fusion.5
  336.6 1.0 convert_add_fusion.5
  337.7 1.9 add_convert_fusion
  339.5 1.2 copy.72
  340.7 4.4 %reduce_sum.40 = bf16[6,128,128]{2,1,0:T(8,128)(2,1)S(1)} reduce(bf16[32,6,128,128]{3,2,1,0:T(8,128)(2,1)} %get-tuple-element.234, bf16[]{:T(256)} %constant.54.clone.1), dimensions={0}, to_apply=%region_7.8 | reduce | flops 3047424 | bytes 6488066 | tf_op jit(solution)/shard_map/reduce_sum | solution.py:88
  346.5 1.2 copy.71
  347.7 2.5 reduce-scatter.2.cloned.1.call-done
  (43 shorter events, 11.9 us)
Async XLA Ops:
  7.2 4.8 %copy-start.5 = (bf16[512,768]{1,0:T(8,128)(2,1)S(1)}, bf16[512,768]{1,0:T(8,128)(2,1)}, u32[]{:S(2)}) copy-start(bf16[512,768]{1,0:T(8,128)(2,1)} %param.10) | copy-start | bytes 2359300
  7.2 96.3 %all-gather.8.cloned.1.call-start = ((), (), s32[]{:S(2)}) async-start(), calls=%async_computation.3 | async-start | bytes 6488064 | tf_op jit(solution)/shard_map/all_gather | solution.py:13
  11.2 195.4 %all-gather.6.cloned.1.call-start = ((), (), s32[]{:S(2)}) async-start(), calls=%async_computation.1 | async-start | bytes 9732096 | tf_op jit(solution)/shard_map/all_gather | solution.py:55
  11.9 293.4 %all-gather.10.cloned.1.call-start = ((), (), s32[]{:S(2)}) async-start(), calls=%async_computation.4 | async-start | bytes 6488064 | tf_op jit(solution)/shard_map/all_gather | solution.py:13
  12.4 1.1 copy-start.7
  13.5 1.7 copy-start
  17.4 86.1 %copy-start.6 = (f32[6,128,128]{2,1,0:T(8,128)S(1)}, f32[6,128,128]{2,1,0:T(8,128)}, u32[]{:S(2)}) copy-start(f32[6,128,128]{2,1,0:T(8,128)} %param.13) | copy-start | bytes 1179652
  206.5 9.6 %copy-start.4 = (f32[6,512,128]{1,2,0:T(8,128)S(1)}, f32[6,512,128]{1,2,0:T(8,128)}, u32[]{:S(2)}) copy-start(f32[6,512,128]{1,2,0:T(8,128)} %fusion.7) | copy-start | bytes 4718596
  219.4 130.8 %reduce-scatter.2.cloned.1.call-start = ((), (), s32[]{:S(2)}) async-start(), calls=%async_computation.2 | async-start | bytes 7077888 | tf_op jit(solution)/shard_map/reduce_scatter | solution.py:60
  232.5 2.4 copy-start.1
  237.2 3.8 %copy-start.2 = (bf16[6,512,512]{2,1,0:T(8,128)(2,1)S(1)}, bf16[6,512,512]{2,1,0:T(8,128)(2,1)}, u32[]{:S(2)}) copy-start(bf16[6,512,512]{2,1,0:T(8,128)(2,1)} %copy-done.1) | copy-start | bytes 9437188
  340.7 5.5 %copy-start.3 = (f32[6,512,128]{1,2,0:T(8,128)S(1)}, f32[6,512,128]{1,2,0:T(8,128)}, u32[]{:S(2)}) copy-start(f32[6,512,128]{1,2,0:T(8,128)} %fusion.11) | copy-start | bytes 4718596
Sparse Core Ops, SparseCore 0:
  11.3 92.1 all-gather.7
  106.1 100.4 all-gather.5
  219.5 85.8 all-gather.9
  308.4 41.7 reduce-scatter.1
